TPU v7x, 32 devices: a whole 2x2x4 slice. The times are simulated.
32 devices in a mesh: dp: 4 (over y, x), vocab: 8 (over z, core).
Axes of the slice: x: 2, y: 2, z: 4, core: 2. Of those that a mesh axis runs over, the one named last changes fastest.
Arguments:
- hidden: bfloat16 [1024, 5120], P('dp')
- head_t: bfloat16 [5120, 19456], P('dp', 'vocab'), may hold values from -0.25 to 0.25
- targets: int32 [1024], P('dp'), may hold values from 0 to 19455
- token_ids: int32 [1024], P('dp'), may hold values from 0 to 19455, as said below
- embed_cot: bfloat16 [1024, 5120], P('dp'), may hold values from -6 to 6
Outputs:
- head_grad: bfloat16 [5120, 19456], P('dp', 'vocab')
- embed_grad: bfloat16 [5120, 19456], P('dp', 'vocab')
- hidden_grad: bfloat16 [1024, 5120], P('vocab', 'dp')
Inputs may be any that keep to these rules, and one draw needn't show every extreme that they name: `token_ids`: among the 256 input ids of one data group, at most 64 lie in any one block of 2432 vocabulary rows that starts at a multiple of 2432; in every group some block holds exactly 64.
All inputs are finite; a program needn't handle non-finite values.
Results may differ from a plain program's by a relative error of at most 0.0033.
Values may be sent and summed in bfloat16 or wider, within the bound.
A program may use at most 128 MiB of HBM per device.

v0:
```python
import jax
import jax.numpy as jnp
from jax import lax
from jax.sharding import PartitionSpec as P


def on_device(hidden, head_t, targets, token_ids, embed_cot):
    width_dev = head_t.shape[1]
    offset = lax.axis_index("vocab") * width_dev
    all_ids = lax.all_gather(token_ids, "dp", axis=0, tiled=True)
    columns = offset + jnp.arange(width_dev, dtype=jnp.int32)[None, :]
    local_hidden, local_cot = (
        lax.all_to_all(hidden, "dp", split_axis=1, concat_axis=0, tiled=True),
        lax.all_to_all(embed_cot, "dp", split_axis=1, concat_axis=0, tiled=True),
    )
    id_hot = (columns == all_ids[:, None]).astype(jnp.bfloat16)
    embed_grad = lax.dot_general(
        local_cot, id_hot, (((0,), (0,)), ((), ())), preferred_element_type=jnp.float32
    ).astype(jnp.bfloat16)
    logits = lax.psum_scatter(
        jnp.dot(local_hidden, head_t, preferred_element_type=jnp.float32),
        "dp",
        scatter_dimension=0,
        tiled=True,
    )
    row_max = lax.pmax(jnp.max(logits, axis=1, keepdims=True), "vocab")
    expo = jnp.exp(logits - row_max)
    row_sum = lax.psum(jnp.sum(expo, axis=1, keepdims=True), "vocab")
    target_hot = (columns == targets[:, None]).astype(jnp.float32)
    dlogits = (expo / row_sum - target_hot).astype(jnp.bfloat16)
    all_grads = lax.all_gather(dlogits, "dp", axis=0, tiled=True)
    head_grad = lax.dot_general(
        local_hidden, all_grads, (((0,), (0,)), ((), ())), preferred_element_type=jnp.float32
    ).astype(jnp.bfloat16)
    hidden_grad = lax.psum_scatter(
        lax.dot_general(
            all_grads, head_t, (((1,), (1,)), ((), ())), preferred_element_type=jnp.float32
        ),
        "vocab",
        scatter_dimension=0,
        tiled=True,
    ).astype(jnp.bfloat16)
    return (head_grad, embed_grad, hidden_grad)


def solution(mesh):
    placed = (P("dp", None), P("dp", "vocab"), P("dp"), P("dp"), P("dp", None))
    return jax.shard_map(
        on_device,
        mesh=mesh,
        in_specs=placed,
        out_specs=(P("dp", "vocab"), P("dp", "vocab"), P("vocab", "dp")),
        check_vma=False,
    )
```

profile of v0, /device:TPU:7, one launch (start us, length us, event | category | flops | bytes accessed | tf_op | source)
XLA Modules:
  0.0 355.9 jit_solution(14743323993973278830)
XLA Ops:
  7.2 0.0 reduce-scatter.3.cloned.1.call-start
  7.2 4.4 %copy.18 = bf16[256,5120]{0,1:T(8,128)(2,1)} copy(bf16[256,5120]{1,0:T(8,128)(2,1)} %param.5) | data formatting | bytes 5242880 | tf_op args[0]
  11.6 32.0 %all_to_all.38 = bf16[256,4,1280]{0,2,1:T(8,128)(2,1)S(1)} all-to-all(bf16[256,4,1280]{0,2,1:T(8,128)(2,1)} %bitcast.22), channel_id=1, replica_groups=mesh['dp'=4,'vocab'=8] {'dp'}, dimensions={1} | all-to-all | bytes 5242880 | tf_op jit(solution)/shard_map/all_to_all | solution.py:13
  43.6 2.6 copy.19
  46.2 12.5 %fusion.8 = f32[1024,2432]{1,0:T(8,128)} fusion(bf16[1024,1280]{1,0:T(8,128)(2,1)} %bitcast.23, bf16[1280,2432]{1,0:T(8,128)(2,1)} %param.6), kind=kOutput, calls=%fused_computation.11 | convolution fusion | flops 6375342080 | bytes 18808832 | tf_op jit(solution)/shard_map/dot_general | solution.py:21
  58.7 0.0 reduce-scatter.3.cloned.1.call-update
  58.8 0.0 copy-start.3
  58.8 0.0 all-gather.3.cloned.1.call-start
  58.8 100.7 %reduce-scatter.3.cloned.1.call-done = f32[256,2432]{1,0:T(8,128)} async-done(((f32[1024,2432]{1,0:T(8,128)}), f32[256,2432]{1,0:T(8,128)}) %reduce-scatter.3.cloned.1.call-update) | async-done | bytes 2490384 | tf_op jit(solution)/shard_map/reduce_scatter | solution.py:20
  159.5 0.0 copy-start
  159.5 2.1 reduce_max.9
  161.6 13.8 %pmax.7 = f32[256]{0:T(256)S(1)} all-reduce(f32[256]{0:T(256)S(1)} %reduce_max.9), channel_id=1, replica_groups=mesh['dp'=4,'vocab'=8] {'vocab'}, use_global_device_ids=true, to_apply=%region_2.0 | all-reduce | flops 256 | bytes 2048 | tf_op jit(solution)/shard_map/pmax | solution.py:26
  175.3 0.0 copy-done
  175.3 0.5 fusion.7
  175.8 16.2 %psum.7 = f32[256]{0:T(256)S(1)} all-reduce(f32[256]{0:T(256)S(1)} %fusion.7), channel_id=1, replica_groups=mesh['dp'=4,'vocab'=8] {'vocab'}, use_global_device_ids=true, to_apply=%region_4.0 | all-reduce | flops 256 | bytes 2048 | tf_op jit(solution)/shard_map/psum | solution.py:28
  192.1 0.0 copy-done.3
  192.1 1.8 subtract_convert_fusion
  193.8 0.0 all-gather.3.cloned.1.call-update
  193.8 0.0 reduce-scatter.5.cloned.1.call-start
  193.9 56.2 %all-gather.3.cloned.1.call-done = bf16[1024,2432]{1,0:T(8,128)(2,1)} async-done(((bf16[256,2432]{1,0:T(8,128)(2,1)}), bf16[1024,2432]{1,0:T(8,128)(2,1)}) %all-gather.3.cloned.1.call-update) | async-done | bytes 4980752 | tf_op jit(solution)/shard_map/all_gather | solution.py:31
  250.1 12.3 %fusion.9 = f32[1024,1280]{1,0:T(8,128)} fusion(bf16[1024,2432]{1,0:T(8,128)(2,1)} %all-gather.3.cloned.1.call-done, bf16[1280,2432]{1,0:T(8,128)(2,1)} %param.6), kind=kOutput, calls=%fused_computation.12 | convolution fusion | flops 6375342080 | bytes 16449536 | tf_op jit(solution)/shard_map/dot_general | solution.py:36
  262.4 0.0 copy-start.1
  262.4 0.0 reduce-scatter.5.cloned.1.call-update
  262.4 1.7 copy-done.1
  264.1 2.5 copy.20
  266.7 0.0 copy-start.4
  266.7 5.0 %all-to-all-start.1 = ((bf16[256,4,1280]{0,2,1:T(8,128)(2,1)}), bf16[256,4,1280]{0,2,1:T(8,128)(2,1)S(1)}, u32[]{:S(2)}, u32[]{:S(2)}) async-start(bf16[256,4,1280]{0,2,1:T(8,128)(2,1)} %bitcast.20), calls=%async_computation.2 | async-start | bytes 5242880 | tf_op jit(solution)/shard_map/all_to_all | solution.py:14
  271.7 0.0 copy-done.4
  271.7 31.4 %all-gather = s32[4,1,256]{2,1,0:T(1,128)S(1)} all-gather(s32[1,1,256]{2,1,0:T(1,128)S(1)} %bitcast.27), channel_id=1, replica_groups=mesh['dp'=4,'vocab'=8] {'dp'}, dimensions={0}, use_global_device_ids=true | all-gather | bytes 5120 | tf_op jit(solution)/shard_map/all_gather | solution.py:10
  303.1 0.0 all-to-all-done.1
  303.1 2.6 copy.21
  305.6 10.9 %fusion.2 = bf16[1280,2432]{0,1:T(8,128)(2,1)} fusion(bf16[1024,1280]{1,0:T(8,128)(2,1)} %bitcast.25, s32[2432]{0:T(1024)S(1)} %iota_add_fusion, s32[1024]{0:T(1024)S(1)} %bitcast.26), kind=kOutput, calls=%fused_computation.4 | convolution fusion | flops 6380945408 | bytes 8861184 | tf_op jit(solution)/shard_map/dot_general | solution.py:17
  316.5 0.0 copy-start.2
  316.5 9.4 %copy.23 = bf16[1280,2432]{1,0:T(8,128)(2,1)} copy(bf16[1280,2432]{0,1:T(8,128)(2,1)} %fusion.2) | data formatting | bytes 12451840
  325.9 0.0 copy-done.2
  325.9 12.3 %fusion.1 = bf16[1280,2432]{0,1:T(8,128)(2,1)} fusion(bf16[1024,2432]{1,0:T(8,128)(2,1)} %all-gather.3.cloned.1.call-done, bf16[1024,1280]{1,0:T(8,128)(2,1)S(1)} %bitcast.24), kind=kOutput, calls=%fused_computation.3 | convolution fusion | flops 6378455040 | bytes 13828096 | tf_op jit(solution)/shard_map/dot_general | solution.py:32
  338.3 9.3 %copy.22 = bf16[1280,2432]{1,0:T(8,128)(2,1)} copy(bf16[1280,2432]{0,1:T(8,128)(2,1)} %fusion.1) | data formatting | bytes 12451840
  347.6 0.0 reduce-scatter.5.cloned.1.call-done
  347.6 1.8 convert_element_type.28
  (1 shorter events, 0.0 us)
Async XLA Ops:
  7.2 152.3 %reduce-scatter.3.cloned.1.call-start = ((), (), s32[]{:S(2)}) async-start(), calls=%async_computation.4 | async-start | bytes 12451840 | tf_op jit(solution)/shard_map/reduce_scatter | solution.py:20
  58.8 133.3 %copy-start.3 = (s32[256]{0:T(256)S(1)}, s32[256]{0:T(256)}, u32[]{:S(2)}) copy-start(s32[256]{0:T(256)} %param.7) | copy-start | bytes 3076
  58.8 191.4 %all-gather.3.cloned.1.call-start = ((), (), s32[]{:S(2)}) async-start(), calls=%async_computation.5 | async-start | bytes 6225920 | tf_op jit(solution)/shard_map/all_gather | solution.py:31
  159.5 15.8 %copy-start = (f32[256,2432]{1,0:T(8,128)S(1)}, f32[256,2432]{1,0:T(8,128)}, u32[]{:S(2)}) copy-start(f32[256,2432]{1,0:T(8,128)} %reduce-scatter.3.cloned.1.call-done) | copy-start | bytes 7471108
  193.8 153.7 %reduce-scatter.5.cloned.1.call-start = ((), (), s32[]{:S(2)}) async-start(), calls=%async_computation.6 | async-start | bytes 5898240 | tf_op jit(solution)/shard_map/reduce_scatter | solution.py:35
  262.4 1.7 copy-start.1
  266.7 5.0 %copy-start.4 = (s32[256]{0:T(256)S(1)}, s32[256]{0:T(256)}, u32[]{:S(2)}) copy-start(s32[256]{0:T(256)} %param.8) | copy-start | bytes 3076
  266.7 36.4 %all-to-all-start.1 = ((bf16[256,4,1280]{0,2,1:T(8,128)(2,1)}), bf16[256,4,1280]{0,2,1:T(8,128)(2,1)S(1)}, u32[]{:S(2)}, u32[]{:S(2)}) async-start(bf16[256,4,1280]{0,2,1:T(8,128)(2,1)} %bitcast.20), calls=%async_computation.2 | async-start | bytes 5242880 | tf_op jit(solution)/shard_map/all_to_all | solution.py:14
  316.5 9.4 %copy-start.2 = (bf16[4,256,1280]{2,1,0:T(8,128)(2,1)S(1)}, bf16[4,256,1280]{2,1,0:T(8,128)(2,1)}, u32[]{:S(2)}) copy-start(bf16[4,256,1280]{2,1,0:T(8,128)(2,1)} %copy.19) | copy-start | bytes 7864324
Sparse Core Ops, SparseCore 0:
  58.9 100.5 reduce-scatter.2
  194.0 56.1 all-gather.2
  262.5 59.0 reduce-scatter.4
where the time goes:
time: 359 us; the launch traced here: 356 us
  waiting for transfers between devices  157 us (44%)
  blocking collectives  93.4 us (26%)
  matrix products  48 us (13%)
  local copies, waits for them, and re-layouts  32.5 us (9%)
  between operations  13.8 us (4%)
  other arithmetic  6.14 us (2%)
  starting transfers between devices  5.16 us (1%)
    reduce_scatter x1, waiting for transfers between devices, on_device(): lax.psum_scatter(jnp.dot(local_hidden, head_t, preferred_element_type=jnp...  101 us
    all_gather x1, waiting for transfers between devices, on_device(): all_grads = lax.all_gather(dlogits, 'dp', axis=0, tiled=True)  56.2 us
    all_to_all x1, blocking collectives, on_device(): lax.all_to_all(hidden, 'dp', split_axis=1, concat_axis=0, tiled=True)  32 us
    all_gather x1, blocking collectives, on_device(): all_ids = lax.all_gather(token_ids, 'dp', axis=0, tiled=True)  31.4 us
    unnamed x14, local copies, waits for them, and re-layouts  27.4 us
    psum x1, blocking collectives, on_device(): row_sum = lax.psum(jnp.sum(expo, axis=1, keepdims=True), 'vocab')  16.2 us
    pmax x1, blocking collectives, on_device(): row_max = lax.pmax(jnp.max(logits, axis=1, keepdims=True), 'vocab')  13.8 us
    dot_general x1, matrix products, on_device(): jnp.dot(local_hidden, head_t, preferred_element_type=jnp.float32)  12.5 us
  transfers between devices with their start and end apart: 4, of which 2 were waited for; matrix products, arithmetic and copies ran while one was open for 13% of the time, Pallas kernels for 0%

commit v1 on v0

v1 whole, which is shorter than its diff:
```python
import functools

import jax
import jax.numpy as jnp
from jax import lax
from jax.experimental import pallas as pl
from jax.experimental.pallas import tpu as pltpu
from jax.sharding import PartitionSpec as P

F32 = jnp.float32
BF16 = jnp.bfloat16
LANE = 128


def column_tiles(start, stop, body):
    full = (stop - start) // 256

    @pl.loop(0, full)
    def _(i):
        body(pl.multiple_of(start + i * 256, 128), 256)

    if (stop - start) % 256:
        body(start + full * 256, (stop - start) % 256)


def core_kernel(
    ndp, nv,
    hidden, cot, head, targets, ids,
    lh_out, lc_out, dl_out, ids_out, hg_out,
    w, lh, lc, idall, part, got, relay, dl, stat, srow, sall, hgp, hgs, hgd, hgr,
    loc, fs, fr, ss, sr, hs, hr, gs, gr,
):
    tok = hidden.shape[0]
    half = tok // 2
    wide, vdev = head.shape
    cut = (vdev // LANE + 1) // 2 * LANE
    rows = hg_out.shape[0]
    pairs = nv // (2 * ndp)
    chips = nv // 2
    me = lax.axis_index("dp")
    vi = lax.axis_index("vocab")
    core = lax.rem(vi, 2)
    chip = lax.div(vi, 2)
    sib = vi + 1 - 2 * core
    px = me + 1 - 2 * lax.rem(me, 2)
    py = lax.rem(me + 2, 4)
    pd = 3 - me

    def send(src, dst, ssem, rsem, dp, vocab):
        return pltpu.make_async_remote_copy(
            src_ref=src, dst_ref=dst, send_sem=ssem, recv_sem=rsem,
            device_id={"dp": dp, "vocab": vocab}, device_id_type=pl.DeviceIdType.MESH,
        )

    load_w = pltpu.make_async_copy(head, w, loc.at[0])
    load_w.start()
    load_h = pltpu.make_async_copy(
        hidden.at[:, pl.ds(pl.multiple_of(me * wide, LANE), wide)], lh.at[me], loc.at[1])
    load_h.start()
    load_c = pltpu.make_async_copy(
        cot.at[:, pl.ds(pl.multiple_of(me * wide, LANE), wide)], lc.at[me], loc.at[2])
    load_c.start()
    load_i = pltpu.make_async_copy(ids, idall.at[me], loc.at[3])
    load_i.start()

    barrier = pltpu.get_barrier_semaphore()
    for p in (px, py, pd):
        pl.semaphore_signal(barrier, inc=1, device_id={"dp": p, "vocab": vi},
                            device_id_type=pl.DeviceIdType.MESH)
    for o in range(1, nv):
        pl.semaphore_signal(barrier, inc=1, device_id={"dp": me, "vocab": lax.rem(vi + o, nv)},
                            device_id_type=pl.DeviceIdType.MESH)
    pl.semaphore_wait(barrier, ndp - 1 + nv - 1)

    mine = pl.ds(pl.multiple_of(core * half, 16), half)
    peers = (pd, px, py)

    def scatter(src, buf, base):
        out = []
        for k, p in enumerate(peers):
            c = send(src.at[mine, pl.ds(pl.multiple_of(p * wide, LANE), wide)],
                     buf.at[me, mine, :], fs.at[base + k], fr.at[base + k], p, vi)
            c.start()
            out.append(c)
        return out

    def share(buf, base, k):
        c = send(buf.at[peers[k], mine, :], buf.at[peers[k], mine, :],
                 fs.at[base + k], fr.at[base + k], me, sib)
        c.start()
        return c

    first = scatter(hidden, lh, 0)
    pending = list(first)
    load_w.wait()
    load_h.wait()

    def logits(slot, group, start, stop):
        def body(c, n):
            part[slot, :, pl.ds(c, n)] = jnp.dot(
                lh[group], w[:, pl.ds(c, n)], preferred_element_type=F32)
        column_tiles(start, stop, body)

    shared = []
    logits(0, me, 0, vdev)
    for k in range(3):
        first[k].wait_recv()
        shared.append(share(lh, 3, k))
    shared[0].wait_recv()
    lo, hi = pl.ds(0, cut), pl.ds(cut, vdev - cut)
    logits(3, pd, 0, cut)
    d_a = send(part.at[3, :, lo], relay.at[:, lo], fs.at[6], fr.at[6], px, vi)
    d_a.start()
    logits(3, pd, cut, vdev)
    d_b = send(part.at[3, :, hi], relay.at[:, hi], fs.at[7], fr.at[7], py, vi)
    d_b.start()
    shared[1].wait_recv()
    logits(1, px, 0, cut)
    x_a = send(part.at[1, :, lo], got.at[0, :, lo], fs.at[8], fr.at[8], px, vi)
    x_a.start()
    shared[2].wait_recv()
    logits(2, py, cut, vdev)
    y_b = send(part.at[2, :, hi], got.at[1, :, hi], fs.at[9], fr.at[9], py, vi)
    y_b.start()
    logits(1, px, cut, vdev)
    logits(2, py, 0, cut)

    out_lh = pltpu.make_async_copy(lh, lh_out, loc.at[1])
    out_lh.start()

    d_a.wait_recv()

    @pl.loop(0, tok // 16)
    def _(i):
        r = pl.ds(pl.multiple_of(i * 16, 16), 16)
        part[2, r, lo] = part[2, r, lo] + relay[r, lo]

    y_a = send(part.at[2, :, lo], got.at[1, :, lo], fs.at[10], fr.at[10], py, vi)
    y_a.start()
    d_b.wait_recv()

    @pl.loop(0, tok // 16)
    def _(i):
        r = pl.ds(pl.multiple_of(i * 16, 16), 16)
        part[1, r, hi] = part[1, r, hi] + relay[r, hi]

    x_b = send(part.at[1, :, hi], got.at[0, :, hi], fs.at[11], fr.at[11], px, vi)
    x_b.start()
    pending += shared + [d_a, d_b, x_a, y_b, y_a, x_b]
    for c in (x_a, y_b, y_a, x_b):
        c.wait_recv()

    load_c.wait()
    load_i.wait()
    moved = scatter(cot, lc, 12)
    pending += moved
    id_moves = []
    for k, p in enumerate(peers):
        c = send(ids, idall.at[me], fs.at[18 + k], fr.at[18 + k], p, vi)
        c.start()
        id_moves.append(c)
    pending += id_moves

    lane = lax.broadcasted_iota(jnp.int32, (16, LANE), 1)

    @pl.loop(0, tok // 16)
    def _(i):
        r = pl.ds(pl.multiple_of(i * 16, 16), 16)
        l = part[0, r, :] + got[0, r, :] + got[1, r, :]
        part[0, r, :] = l
        m = jnp.max(l, axis=1, keepdims=True)
        s = jnp.sum(jnp.exp(l - m), axis=1, keepdims=True)
        stat[r, :] = jnp.where(lane == 0, m, s)

    srow[...] = stat[...].T[:8]
    stats = []
    for o in range(1, nv):
        c = send(srow, sall.at[o], ss.at[o], sr.at[o], me, lax.rem(vi + o, nv))
        c.start()
        stats.append(c)
    sall[0] = srow[...]
    for c in stats:
        c.wait_recv()
    top = sall[0, 0:1, :]
    for o in range(1, nv):
        top = jnp.maximum(top, sall[o, 0:1, :])
    total = jnp.zeros_like(top)
    for o in range(nv):
        total = total + sall[o, 1:2, :] * jnp.exp(sall[o, 0:1, :] - top)
    sub = lax.broadcasted_iota(jnp.int32, (LANE, tok), 0)
    stat[...] = jnp.where(sub == 0, top, total).T
    for c in stats:
        c.wait_send()

    shift = vi * vdev

    @pl.loop(0, tok // 16)
    def _(i):
        r = pl.ds(pl.multiple_of(i * 16, 16), 16)
        m = stat[r, 0:1]
        s = stat[r, 1:2]
        cols = lax.broadcasted_iota(jnp.int32, (16, vdev), 1) + shift
        hot = (cols == targets[r, :]).astype(F32)
        dl[me, r, :] = (jnp.exp(part[0, r, :] - m) / s - hot).astype(BF16)

    g_x = send(dl.at[me], dl.at[me], fs.at[21], fr.at[21], px, vi)
    g_y = send(dl.at[me], dl.at[me], fs.at[22], fr.at[22], py, vi)
    g_x.start()
    g_y.start()
    pending += [g_x, g_y]

    hg_sends = []

    def hidden_grad(step, g):
        def body(c, n):
            hgp[step, :, pl.ds(c, n)] = lax.dot_general(
                dl[g], w[pl.ds(c, n), :], (((1,), (1,)), ((), ())),
                preferred_element_type=F32).astype(BF16)
        column_tiles(0, wide, body)
        out = []
        for i in range(pairs):
            away = pl.ds(pl.multiple_of((2 * i + 1 - core) * rows, 16), rows)
            c = send(hgp.at[step, away, :], hgs.at[step, i],
                     hs.at[step * pairs + i], hr.at[step * pairs + i], me, sib)
            c.start()
            out.append(c)
        return out

    def forward(step, g, out):
        for i in range(pairs):
            out[i].wait_recv()
            keep = pl.ds(pl.multiple_of((2 * i + core) * rows, 16), rows)
            hgd[step, i] = (hgp[step, keep, :].astype(F32) + hgs[step, i].astype(F32)).astype(BF16)
            dest = g * pairs + i
            slot = lax.rem(chip - dest + chips, chips)

            @pl.when(slot != 0)
            def _():
                send(hgd.at[step, i], hgr.at[slot], gs.at[step * pairs + i], gr.at[slot],
                     me, 2 * dest + core).start()

            @pl.when(slot == 0)
            def _():
                hgr[0] = hgd[step, i]

            hg_sends.append((step, i, slot, dest))

    s0 = hidden_grad(0, me)
    a, b = pl.ds(0, half), pl.ds(half, half)
    g_x.wait_recv()
    r_x = send(dl.at[px, a, :], dl.at[px, a, :], fs.at[23], fr.at[23], py, vi)
    r_x.start()
    g_y.wait_recv()
    r_y = send(dl.at[py, b, :], dl.at[py, b, :], fs.at[24], fr.at[24], px, vi)
    r_y.start()
    pending += [r_x, r_y]
    forward(0, me, s0)
    s1 = hidden_grad(1, px)
    for k in range(3):
        moved[k].wait_recv()
        c = share(lc, 15, k)
        pending.append(c)
        shared.append(c)
    forward(1, px, s1)
    s2 = hidden_grad(2, py)
    forward(2, py, s2)
    for c in shared[3:]:
        c.wait_recv()
    for c in id_moves:
        c.wait_recv()
    out_lc = pltpu.make_async_copy(lc, lc_out, loc.at[2])
    out_lc.start()
    out_id = pltpu.make_async_copy(idall, ids_out, loc.at[3])
    out_id.start()
    r_x.wait_recv()
    r_y.wait_recv()
    out_dl = pltpu.make_async_copy(dl, dl_out, loc.at[0])
    out_dl.start()
    s3 = hidden_grad(3, pd)
    forward(3, pd, s3)

    for o in range(1, chips):
        send(hgd.at[0, 0], hgr.at[o], gs.at[0], gr.at[o], me, sib).wait_recv()
    acc = hgr[0].astype(F32)
    for o in range(1, chips):
        acc = acc + hgr[o].astype(F32)
    hg_out[...] = acc.astype(BF16)

    for step, i, slot, dest in hg_sends:
        @pl.when(slot != 0)
        def _():
            send(hgd.at[step, i], hgr.at[slot], gs.at[step * pairs + i], gr.at[slot],
                 me, 2 * dest + core).wait_send()
    for c in s0 + s1 + s2 + s3 + pending:
        c.wait_send()
    for c in (out_lh, out_lc, out_id, out_dl):
        c.wait()


def core_call(ndp, nv, hidden, cot, head, targets, ids):
    tok, full = hidden.shape
    wide, vdev = head.shape
    rows = tok * ndp // nv
    pairs = nv // (2 * ndp)
    dma = pltpu.SemaphoreType.DMA
    anyspec = pl.BlockSpec(memory_space=pl.ANY)
    vspec = pl.BlockSpec(memory_space=pltpu.VMEM)
    return pl.pallas_call(
        functools.partial(core_kernel, ndp, nv),
        out_shape=(
            jax.ShapeDtypeStruct((ndp, tok, wide), BF16),
            jax.ShapeDtypeStruct((ndp, tok, wide), BF16),
            jax.ShapeDtypeStruct((ndp, tok, vdev), BF16),
            jax.ShapeDtypeStruct((ndp, 8, tok), jnp.int32),
            jax.ShapeDtypeStruct((rows, wide), BF16),
        ),
        in_specs=[anyspec, anyspec, anyspec, vspec, anyspec],
        out_specs=(anyspec, anyspec, anyspec, anyspec, vspec),
        scratch_shapes=[
            pltpu.VMEM((wide, vdev), BF16),
            pltpu.VMEM((ndp, tok, wide), BF16),
            pltpu.VMEM((ndp, tok, wide), BF16),
            pltpu.VMEM((ndp, 8, tok), jnp.int32),
            pltpu.VMEM((4, tok, vdev), F32),
            pltpu.VMEM((2, tok, vdev), F32),
            pltpu.VMEM((tok, vdev), F32),
            pltpu.VMEM((ndp, tok, vdev), BF16),
            pltpu.VMEM((tok, LANE), F32),
            pltpu.VMEM((8, tok), F32),
            pltpu.VMEM((nv, 8, tok), F32),
            pltpu.VMEM((4, tok, wide), BF16),
            pltpu.VMEM((4, pairs, rows, wide), BF16),
            pltpu.VMEM((4, pairs, rows, wide), BF16),
            pltpu.VMEM((nv // 2, rows, wide), BF16),
            dma((4,)), dma((25,)), dma((25,)), dma((nv,)), dma((nv,)),
            dma((4 * pairs,)), dma((4 * pairs,)), dma((4 * pairs,)), dma((nv // 2,)),
        ],
        compiler_params=pltpu.CompilerParams(
            collective_id=0, has_side_effects=True, vmem_limit_bytes=64000000),
        name="core",
    )(hidden, cot, head, targets, ids)


def grad_kernel(a_ref, b_ref, o_ref):
    o_ref[...] = lax.dot_general(
        a_ref[...], b_ref[...], (((0,), (0,)), ((), ())),
        preferred_element_type=F32).astype(BF16)


def head_grad_call(lh, dl):
    n, wide = lh.shape
    vdev = dl.shape[1]
    return pl.pallas_call(
        grad_kernel,
        grid=(wide // 256,),
        out_shape=jax.ShapeDtypeStruct((wide, vdev), BF16),
        in_specs=[pl.BlockSpec((n, 256), lambda i: (0, i)),
                  pl.BlockSpec((n, vdev), lambda i: (0, 0))],
        out_specs=pl.BlockSpec((256, vdev), lambda i: (i, 0)),
        name="head_grad",
    )(lh, dl)


def embed_kernel(vdev, a_ref, id_ref, o_ref, hot):
    @pl.when(pl.program_id(0) == 0)
    def _():
        shift = lax.axis_index("vocab") * vdev

        @pl.loop(0, hot.shape[0] // 16)
        def _(i):
            r = pl.ds(pl.multiple_of(i * 16, 16), 16)
            cols = lax.broadcasted_iota(jnp.int32, (16, vdev), 1) + shift
            hot[r, :] = (cols == id_ref[r, :]).astype(F32).astype(BF16)

    grad_kernel(a_ref, hot, o_ref)


def embed_grad_call(lc, ids, vdev):
    n, wide = lc.shape
    return pl.pallas_call(
        functools.partial(embed_kernel, vdev),
        grid=(wide // 256,),
        out_shape=jax.ShapeDtypeStruct((wide, vdev), BF16),
        in_specs=[pl.BlockSpec((n, 256), lambda i: (0, i)),
                  pl.BlockSpec((n, 1), lambda i: (0, 0))],
        out_specs=pl.BlockSpec((256, vdev), lambda i: (i, 0)),
        scratch_shapes=[pltpu.VMEM((n, vdev), BF16)],
        name="embed_grad",
    )(lc, ids)


def on_device(ndp, nv, hidden, head_t, targets, token_ids, embed_cot):
    tok = hidden.shape[0]
    wide, vdev = head_t.shape
    ids8 = jnp.broadcast_to(token_ids[None, :], (8, tok))
    lh, lc, dl, ids, hidden_grad = core_call(
        ndp, nv, hidden, embed_cot, head_t, targets[:, None], ids8)
    n = ndp * tok
    head_grad = head_grad_call(lh.reshape(n, wide), dl.reshape(n, vdev))
    embed_grad = embed_grad_call(lc.reshape(n, wide), ids[:, 0, :].reshape(n, 1), vdev)
    return head_grad, embed_grad, hidden_grad


def solution(mesh):
    placed = (P("dp", None), P("dp", "vocab"), P("dp"), P("dp"), P("dp", None))
    return jax.shard_map(
        functools.partial(on_device, mesh.shape["dp"], mesh.shape["vocab"]),
        mesh=mesh,
        in_specs=placed,
        out_specs=(P("dp", "vocab"), P("dp", "vocab"), P("vocab", "dp")),
        check_vma=False,
    )
```

time: 359 us -> 224 us (0.62)
  Pallas kernels: 0 us -> 218 us
  waiting for transfers between devices: 157 us -> 0 us
  blocking collectives: 93.4 us -> 0 us
  matrix products: 48 us -> 0 us
  local copies, waits for them, and re-layouts: 32.5 us -> 5.3 us
  between operations: 13.8 us -> 0.64 us
  other arithmetic: 6.14 us -> 0 us
  starting transfers between devices: 5.16 us -> 0 us
    pallas_call x0 -> x3, Pallas kernels: none -> 218 us  [the longest x1 191 us: core_call(): pl.pallas_call(functools.partial(core_kernel, ndp, nv), out_shape=(jax.Sh...]
    reduce_scatter x2 -> x0, waiting for transfers between devices: 101 us -> none  [the longest x1 101 us: on_device(): lax.psum_scatter(jnp.dot(local_hidden, head_t, preferred_element_type=jnp...]
    all_gather x1 -> x0, waiting for transfers between devices: 56.2 us -> none  [on_device(): all_grads = lax.all_gather(dlogits, 'dp', axis=0, tiled=True)]
    dot_general x4 -> x0, matrix products: 48 us -> none  [the longest x1 12.5 us: on_device(): jnp.dot(local_hidden, head_t, preferred_element_type=jnp.float32)]
    all_to_all x1 -> x0, blocking collectives: 32 us -> none  [on_device(): lax.all_to_all(hidden, 'dp', split_axis=1, concat_axis=0, tiled=True)]
    all_gather x1 -> x0, blocking collectives: 31.4 us -> none  [on_device(): all_ids = lax.all_gather(token_ids, 'dp', axis=0, tiled=True)]
    unnamed x14 -> x3, local copies, waits for them, and re-layouts: 27.4 us -> 0.73 us
    psum x1 -> x0, blocking collectives: 16.2 us -> none  [on_device(): row_sum = lax.psum(jnp.sum(expo, axis=1, keepdims=True), 'vocab')]
  transfers between devices with their start and end apart: 4 -> 0, of which waited for: 2 -> 0; matrix products, arithmetic and copies ran while one was open for 13% -> 0% of each run, Pallas kernels for 0% -> 0%
where the time goes in v1:
time: 224 us; the launch traced here: 223 us
  Pallas kernels  218 us (97%)
  local copies, waits for them, and re-layouts  5.3 us (2%)
    pallas_call x1, Pallas kernels, core_call(): pl.pallas_call(functools.partial(core_kernel, ndp, nv), out_shape=(jax.Sh...  191 us
    pallas_call x1, Pallas kernels, embed_grad_call(): pl.pallas_call(functools.partial(embed_kernel, vdev), grid=(wide // 256,)...  15.5 us
    pallas_call x1, Pallas kernels, head_grad_call(): pl.pallas_call(grad_kernel, grid=(wide // 256,), out_shape=jax.ShapeDtype...  11.4 us

profile of v1, /device:TPU:7, one launch (start us, length us, event | category | flops | bytes accessed | tf_op | source)
XLA Modules:
  0.0 223.5 jit_solution(4683430931528164008)
XLA Ops:
  0.6 1.3 broadcast_in_dim.10.ids
  1.9 1.5 copy.8.targets
  3.4 190.6 %core.1 = (bf16[4,256,1280]{2,1,0:T(8,128)(2,1)}, bf16[4,256,1280]{2,1,0:T(8,128)(2,1)}, bf16[4,256,2432]{2,1,0:T(8,128)(2,1)}, s32[4,8,256]{2,1,0:T(8,128)}, bf16[128,1280]{1,0:T(8,128)(2,1)}) custom-call(bf16[256,5120]{1,0:T(8,128)(2,1)} %hidden.1, bf16[256,5120]{1,0:T(8,128)(2,1)} %cot.1, bf16[1280,2432]{1,0:T(8,128)(2,1)} %head.1, ...), custom_call_target="tpu_custom_call" | custom-call | tf_op jit(solution)/shard_map/core/pallas_call | solution.py:308
  194.0 11.4 %head_grad.1 = bf16[1280,2432]{1,0:T(8,128)(2,1)} custom-call(bf16[1024,1280]{1,0:T(8,128)(2,1)} %bitcast.7, bf16[1024,2432]{1,0:T(8,128)(2,1)} %bitcast.5), custom_call_target="tpu_custom_call" | custom-call | tf_op jit(solution)/shard_map/head_grad/pallas_call | solution.py:353
  205.5 0.0 copy-start
  205.5 0.8 slice.3
  206.3 1.0 copy.9.id_ref
  207.3 15.5 %embed_grad.1 = bf16[1280,2432]{1,0:T(8,128)(2,1)} custom-call(bf16[1024,1280]{1,0:T(8,128)(2,1)} %bitcast.6, s32[1024,1]{1,0:T(8,128)} %copy.9.id_ref), custom_call_target="tpu_custom_call" | custom-call | tf_op jit(solution)/shard_map/embed_grad/pallas_call | solution.py:380
  222.8 0.0 copy-done
  222.8 0.7 copy.11
Async XLA Ops:
  205.5 17.3 %copy-start = (bf16[128,1280]{1,0:T(8,128)(2,1)S(1)}, bf16[128,1280]{1,0:T(8,128)(2,1)}, u32[]{:S(2)}) copy-start(bf16[128,1280]{1,0:T(8,128)(2,1)} %get-tuple-element.18) | copy-start | bytes 983044

commit v2 on v1

--- a/solution.py
+++ b/solution.py
@@ -27,7 +27,7 @@
     ndp, nv,
     hidden, cot, head, targets, ids,
     lh_out, lc_out, dl_out, ids_out, hg_out,
-    w, lh, lc, idall, part, got, relay, dl, stat, srow, sall, hgp, hgs, hgd, hgr,
+    w, lh, cotv, sel, pick, lc, idsend, idall, tcol, part, got, relay, dl, stat, srow, sall, hgp, hgs, hgd, hgr,
     loc, fs, fr, ss, sr, hs, hr, gs, gr,
 ):
     tok = hidden.shape[0]
@@ -35,6 +35,8 @@
     wide, vdev = head.shape
     cut = (vdev // LANE + 1) // 2 * LANE
     rows = hg_out.shape[0]
+    bound = lc.shape[1]
+    quarter = tok // 4
     pairs = nv // (2 * ndp)
     chips = nv // 2
     me = lax.axis_index("dp")
@@ -42,6 +44,8 @@
     core = lax.rem(vi, 2)
     chip = lax.div(vi, 2)
     sib = vi + 1 - 2 * core
+    odd = lax.rem(chip, 2)
+    zp = vi + 2 - 4 * odd
     px = me + 1 - 2 * lax.rem(me, 2)
     py = lax.rem(me + 2, 4)
     pd = 3 - me
@@ -57,11 +61,8 @@
     load_h = pltpu.make_async_copy(
         hidden.at[:, pl.ds(pl.multiple_of(me * wide, LANE), wide)], lh.at[me], loc.at[1])
     load_h.start()
-    load_c = pltpu.make_async_copy(
-        cot.at[:, pl.ds(pl.multiple_of(me * wide, LANE), wide)], lc.at[me], loc.at[2])
+    load_c = pltpu.make_async_copy(cot, cotv, loc.at[2])
     load_c.start()
-    load_i = pltpu.make_async_copy(ids, idall.at[me], loc.at[3])
-    load_i.start()
 
     barrier = pltpu.get_barrier_semaphore()
     for p in (px, py, pd):
@@ -72,26 +73,35 @@
                             device_id_type=pl.DeviceIdType.MESH)
     pl.semaphore_wait(barrier, ndp - 1 + nv - 1)
 
-    mine = pl.ds(pl.multiple_of(core * half, 16), half)
+    mine = pl.ds(pl.multiple_of((2 * odd + core) * quarter, 16), quarter)
+    theirs = pl.ds(pl.multiple_of((2 - 2 * odd + core) * quarter, 16), quarter)
     peers = (pd, px, py)
 
-    def scatter(src, buf, base):
+    first = []
+    for k, p in enumerate(peers):
+        c = send(hidden.at[mine, pl.ds(pl.multiple_of(p * wide, LANE), wide)],
+                 lh.at[me, mine, :], fs.at[k], fr.at[k], p, vi)
+        c.start()
+        first.append(c)
+    pending = list(first)
+
+    def share(k):
         out = []
-        for k, p in enumerate(peers):
-            c = send(src.at[mine, pl.ds(pl.multiple_of(p * wide, LANE), wide)],
-                     buf.at[me, mine, :], fs.at[base + k], fr.at[base + k], p, vi)
+        first[k].wait_recv()
+        for dst, n in ((zp, 0), (sib, 1)):
+            c = send(lh.at[peers[k], mine, :], lh.at[peers[k], mine, :],
+                     fs.at[3 + 3 * k + n], fr.at[3 + 3 * k + n], me, dst)
             c.start()
             out.append(c)
         return out
 
-    def share(buf, base, k):
-        c = send(buf.at[peers[k], mine, :], buf.at[peers[k], mine, :],
-                 fs.at[base + k], fr.at[base + k], me, sib)
+    def relay_on(k, out):
+        out[0].wait_recv()
+        c = send(lh.at[peers[k], theirs, :], lh.at[peers[k], theirs, :],
+                 fs.at[5 + 3 * k], fr.at[5 + 3 * k], me, sib)
         c.start()
-        return c
-
-    first = scatter(hidden, lh, 0)
-    pending = list(first)
+        out.append(c)
+
     load_w.wait()
     load_h.wait()
 
@@ -101,32 +111,66 @@
                 lh[group], w[:, pl.ds(c, n)], preferred_element_type=F32)
         column_tiles(start, stop, body)
 
-    shared = []
-    logits(0, me, 0, vdev)
+    logits(0, me, 0, cut)
+    shared = [share(0), share(1), share(2)]
+    logits(0, me, cut, vdev)
     for k in range(3):
-        first[k].wait_recv()
-        shared.append(share(lh, 3, k))
-    shared[0].wait_recv()
+        relay_on(k, shared[k])
+
+    def arrived(k):
+        shared[k][1].wait_recv()
+        shared[k][2].wait_recv()
+
+    arrived(0)
     lo, hi = pl.ds(0, cut), pl.ds(cut, vdev - cut)
     logits(3, pd, 0, cut)
-    d_a = send(part.at[3, :, lo], relay.at[:, lo], fs.at[6], fr.at[6], px, vi)
+    d_a = send(part.at[3, :, lo], relay.at[:, lo], fs.at[12], fr.at[12], px, vi)
     d_a.start()
     logits(3, pd, cut, vdev)
-    d_b = send(part.at[3, :, hi], relay.at[:, hi], fs.at[7], fr.at[7], py, vi)
+    d_b = send(part.at[3, :, hi], relay.at[:, hi], fs.at[13], fr.at[13], py, vi)
     d_b.start()
-    shared[1].wait_recv()
+    arrived(1)
     logits(1, px, 0, cut)
-    x_a = send(part.at[1, :, lo], got.at[0, :, lo], fs.at[8], fr.at[8], px, vi)
+    x_a = send(part.at[1, :, lo], got.at[0, :, lo], fs.at[14], fr.at[14], px, vi)
     x_a.start()
-    shared[2].wait_recv()
+    arrived(2)
     logits(2, py, cut, vdev)
-    y_b = send(part.at[2, :, hi], got.at[1, :, hi], fs.at[9], fr.at[9], py, vi)
+    y_b = send(part.at[2, :, hi], got.at[1, :, hi], fs.at[15], fr.at[15], py, vi)
     y_b.start()
     logits(1, px, cut, vdev)
     logits(2, py, 0, cut)
 
     out_lh = pltpu.make_async_copy(lh, lh_out, loc.at[1])
     out_lh.start()
+
+    tcol[...] = jnp.broadcast_to(targets[...].astype(F32), (LANE, tok)).T
+    place = jnp.broadcast_to(ids[...].astype(F32), (LANE, tok)).T - (vi * vdev).astype(F32)
+    inside = jnp.logical_and(place >= 0, place < vdev)
+    before = (lax.broadcasted_iota(jnp.int32, (tok, tok), 0)
+              > lax.broadcasted_iota(jnp.int32, (tok, tok), 1)).astype(F32).astype(BF16)
+    rank = jnp.dot(before, inside.astype(F32).astype(BF16), preferred_element_type=F32)
+    slot_no = lax.broadcasted_iota(jnp.int32, (tok, LANE), 1).astype(F32)
+    sel[...] = jnp.logical_and(rank == slot_no, inside).astype(F32).astype(BF16)
+    mark = jnp.where(inside, place + 1, 0.0)
+    high = jnp.floor(mark / 64)
+    low = mark - 64 * high
+
+    def squeeze(x):
+        return lax.dot_general(sel[...], x, (((0,), (0,)), ((), ())),
+                               preferred_element_type=F32)[:bound]
+
+    idsend[...] = 64 * squeeze(high.astype(BF16)) + squeeze(low.astype(BF16)) - 1
+    load_c.wait()
+
+    def compact(c, n):
+        pick[:, pl.ds(c, n)] = squeeze(cotv[:, pl.ds(c, n)]).astype(BF16)
+
+    column_tiles(0, ndp * wide, compact)
+    load_p = pltpu.make_async_copy(
+        pick.at[:, pl.ds(pl.multiple_of(me * wide, LANE), wide)], lc.at[me], loc.at[2])
+    load_p.start()
+    load_i = pltpu.make_async_copy(idsend, idall.at[me], loc.at[3])
+    load_i.start()
 
     d_a.wait_recv()
 
@@ -135,7 +179,7 @@
         r = pl.ds(pl.multiple_of(i * 16, 16), 16)
         part[2, r, lo] = part[2, r, lo] + relay[r, lo]
 
-    y_a = send(part.at[2, :, lo], got.at[1, :, lo], fs.at[10], fr.at[10], py, vi)
+    y_a = send(part.at[2, :, lo], got.at[1, :, lo], fs.at[16], fr.at[16], py, vi)
     y_a.start()
     d_b.wait_recv()
 
@@ -144,22 +188,24 @@
         r = pl.ds(pl.multiple_of(i * 16, 16), 16)
         part[1, r, hi] = part[1, r, hi] + relay[r, hi]
 
-    x_b = send(part.at[1, :, hi], got.at[0, :, hi], fs.at[11], fr.at[11], px, vi)
+    x_b = send(part.at[1, :, hi], got.at[0, :, hi], fs.at[17], fr.at[17], px, vi)
     x_b.start()
-    pending += shared + [d_a, d_b, x_a, y_b, y_a, x_b]
+    pending += shared[0] + shared[1] + shared[2] + [d_a, d_b, x_a, y_b, y_a, x_b]
     for c in (x_a, y_b, y_a, x_b):
         c.wait_recv()
 
-    load_c.wait()
+    load_p.wait()
     load_i.wait()
-    moved = scatter(cot, lc, 12)
+    moved = []
+    for k, p in enumerate(peers):
+        c = send(pick.at[:, pl.ds(pl.multiple_of(p * wide, LANE), wide)], lc.at[me],
+                 fs.at[18 + k], fr.at[18 + k], p, vi)
+        c.start()
+        moved.append(c)
+        c = send(idsend, idall.at[me], fs.at[21 + k], fr.at[21 + k], p, vi)
+        c.start()
+        moved.append(c)
     pending += moved
-    id_moves = []
-    for k, p in enumerate(peers):
-        c = send(ids, idall.at[me], fs.at[18 + k], fr.at[18 + k], p, vi)
-        c.start()
-        id_moves.append(c)
-    pending += id_moves
 
     lane = lax.broadcasted_iota(jnp.int32, (16, LANE), 1)
 
@@ -200,11 +246,11 @@
         m = stat[r, 0:1]
         s = stat[r, 1:2]
         cols = lax.broadcasted_iota(jnp.int32, (16, vdev), 1) + shift
-        hot = (cols == targets[r, :]).astype(F32)
+        hot = (cols == tcol[r, 0:1].astype(jnp.int32)).astype(F32)
         dl[me, r, :] = (jnp.exp(part[0, r, :] - m) / s - hot).astype(BF16)
 
-    g_x = send(dl.at[me], dl.at[me], fs.at[21], fr.at[21], px, vi)
-    g_y = send(dl.at[me], dl.at[me], fs.at[22], fr.at[22], py, vi)
+    g_x = send(dl.at[me], dl.at[me], fs.at[24], fr.at[24], px, vi)
+    g_y = send(dl.at[me], dl.at[me], fs.at[25], fr.at[25], py, vi)
     g_x.start()
     g_y.start()
     pending += [g_x, g_y]
@@ -215,7 +261,7 @@
         def body(c, n):
             hgp[step, :, pl.ds(c, n)] = lax.dot_general(
                 dl[g], w[pl.ds(c, n), :], (((1,), (1,)), ((), ())),
-                preferred_element_type=F32).astype(BF16)
+                preferred_element_type=F32)
         column_tiles(0, wide, body)
         out = []
         for i in range(pairs):
@@ -230,7 +276,7 @@
         for i in range(pairs):
             out[i].wait_recv()
             keep = pl.ds(pl.multiple_of((2 * i + core) * rows, 16), rows)
-            hgd[step, i] = (hgp[step, keep, :].astype(F32) + hgs[step, i].astype(F32)).astype(BF16)
+            hgd[step, i] = (hgp[step, keep, :] + hgs[step, i]).astype(BF16)
             dest = g * pairs + i
             slot = lax.rem(chip - dest + chips, chips)
 
@@ -248,25 +294,18 @@
     s0 = hidden_grad(0, me)
     a, b = pl.ds(0, half), pl.ds(half, half)
     g_x.wait_recv()
-    r_x = send(dl.at[px, a, :], dl.at[px, a, :], fs.at[23], fr.at[23], py, vi)
+    r_x = send(dl.at[px, a, :], dl.at[px, a, :], fs.at[26], fr.at[26], py, vi)
     r_x.start()
     g_y.wait_recv()
-    r_y = send(dl.at[py, b, :], dl.at[py, b, :], fs.at[24], fr.at[24], px, vi)
+    r_y = send(dl.at[py, b, :], dl.at[py, b, :], fs.at[27], fr.at[27], px, vi)
     r_y.start()
     pending += [r_x, r_y]
     forward(0, me, s0)
     s1 = hidden_grad(1, px)
-    for k in range(3):
-        moved[k].wait_recv()
-        c = share(lc, 15, k)
-        pending.append(c)
-        shared.append(c)
     forward(1, px, s1)
     s2 = hidden_grad(2, py)
     forward(2, py, s2)
-    for c in shared[3:]:
-        c.wait_recv()
-    for c in id_moves:
+    for c in moved:
         c.wait_recv()
     out_lc = pltpu.make_async_copy(lc, lc_out, loc.at[2])
     out_lc.start()
@@ -302,6 +341,7 @@
     wide, vdev = head.shape
     rows = tok * ndp // nv
     pairs = nv // (2 * ndp)
+    bound = 2 * tok // nv
     dma = pltpu.SemaphoreType.DMA
     anyspec = pl.BlockSpec(memory_space=pl.ANY)
     vspec = pl.BlockSpec(memory_space=pltpu.VMEM)
@@ -309,18 +349,23 @@
         functools.partial(core_kernel, ndp, nv),
         out_shape=(
             jax.ShapeDtypeStruct((ndp, tok, wide), BF16),
-            jax.ShapeDtypeStruct((ndp, tok, wide), BF16),
+            jax.ShapeDtypeStruct((ndp, bound, wide), BF16),
             jax.ShapeDtypeStruct((ndp, tok, vdev), BF16),
-            jax.ShapeDtypeStruct((ndp, 8, tok), jnp.int32),
+            jax.ShapeDtypeStruct((ndp, bound, LANE), F32),
             jax.ShapeDtypeStruct((rows, wide), BF16),
         ),
-        in_specs=[anyspec, anyspec, anyspec, vspec, anyspec],
+        in_specs=[anyspec, anyspec, anyspec, vspec, vspec],
         out_specs=(anyspec, anyspec, anyspec, anyspec, vspec),
         scratch_shapes=[
             pltpu.VMEM((wide, vdev), BF16),
             pltpu.VMEM((ndp, tok, wide), BF16),
-            pltpu.VMEM((ndp, tok, wide), BF16),
-            pltpu.VMEM((ndp, 8, tok), jnp.int32),
+            pltpu.VMEM((tok, full), BF16),
+            pltpu.VMEM((tok, LANE), BF16),
+            pltpu.VMEM((bound, full), BF16),
+            pltpu.VMEM((ndp, bound, wide), BF16),
+            pltpu.VMEM((bound, LANE), F32),
+            pltpu.VMEM((ndp, bound, LANE), F32),
+            pltpu.VMEM((tok, LANE), F32),
             pltpu.VMEM((4, tok, vdev), F32),
             pltpu.VMEM((2, tok, vdev), F32),
             pltpu.VMEM((tok, vdev), F32),
@@ -328,11 +373,11 @@
             pltpu.VMEM((tok, LANE), F32),
             pltpu.VMEM((8, tok), F32),
             pltpu.VMEM((nv, 8, tok), F32),
-            pltpu.VMEM((4, tok, wide), BF16),
-            pltpu.VMEM((4, pairs, rows, wide), BF16),
+            pltpu.VMEM((4, tok, wide), F32),
+            pltpu.VMEM((4, pairs, rows, wide), F32),
             pltpu.VMEM((4, pairs, rows, wide), BF16),
             pltpu.VMEM((nv // 2, rows, wide), BF16),
-            dma((4,)), dma((25,)), dma((25,)), dma((nv,)), dma((nv,)),
+            dma((4,)), dma((28,)), dma((28,)), dma((nv,)), dma((nv,)),
             dma((4 * pairs,)), dma((4 * pairs,)), dma((4 * pairs,)), dma((nv // 2,)),
         ],
         compiler_params=pltpu.CompilerParams(
@@ -364,13 +409,11 @@
 def embed_kernel(vdev, a_ref, id_ref, o_ref, hot):
     @pl.when(pl.program_id(0) == 0)
     def _():
-        shift = lax.axis_index("vocab") * vdev
-
         @pl.loop(0, hot.shape[0] // 16)
         def _(i):
             r = pl.ds(pl.multiple_of(i * 16, 16), 16)
-            cols = lax.broadcasted_iota(jnp.int32, (16, vdev), 1) + shift
-            hot[r, :] = (cols == id_ref[r, :]).astype(F32).astype(BF16)
+            cols = lax.broadcasted_iota(jnp.int32, (16, vdev), 1)
+            hot[r, :] = (cols == id_ref[r, 0:1].astype(jnp.int32)).astype(F32).astype(BF16)
 
     grad_kernel(a_ref, hot, o_ref)
 
@@ -382,7 +425,7 @@
         grid=(wide // 256,),
         out_shape=jax.ShapeDtypeStruct((wide, vdev), BF16),
         in_specs=[pl.BlockSpec((n, 256), lambda i: (0, i)),
-                  pl.BlockSpec((n, 1), lambda i: (0, 0))],
+                  pl.BlockSpec((n, LANE), lambda i: (0, 0))],
         out_specs=pl.BlockSpec((256, vdev), lambda i: (i, 0)),
         scratch_shapes=[pltpu.VMEM((n, vdev), BF16)],
         name="embed_grad",
@@ -392,12 +435,12 @@
 def on_device(ndp, nv, hidden, head_t, targets, token_ids, embed_cot):
     tok = hidden.shape[0]
     wide, vdev = head_t.shape
-    ids8 = jnp.broadcast_to(token_ids[None, :], (8, tok))
     lh, lc, dl, ids, hidden_grad = core_call(
-        ndp, nv, hidden, embed_cot, head_t, targets[:, None], ids8)
+        ndp, nv, hidden, embed_cot, head_t, targets[None, :], token_ids[None, :])
     n = ndp * tok
     head_grad = head_grad_call(lh.reshape(n, wide), dl.reshape(n, vdev))
-    embed_grad = embed_grad_call(lc.reshape(n, wide), ids[:, 0, :].reshape(n, 1), vdev)
+    slots = lc.shape[0] * lc.shape[1]
+    embed_grad = embed_grad_call(lc.reshape(slots, wide), ids.reshape(slots, LANE), vdev)
     return head_grad, embed_grad, hidden_grad
 
 

time: 224 us -> 207 us (0.924)
  Pallas kernels: 218 us -> 206 us
  local copies, waits for them, and re-layouts: 5.3 us -> 0.73 us
    pallas_call x1, Pallas kernels: 15.5 us -> 7.18 us  [embed_grad_call(): pl.pallas_call(functools.partial(embed_kernel, vdev), grid=(wide // 256,)...]
    pallas_call x1, Pallas kernels: 191 us -> 187 us  [core_call(): pl.pallas_call(functools.partial(core_kernel, ndp, nv), out_shape=(jax.Sh...]
    broadcast_in_dim x2 -> x0, local copies, waits for them, and re-layouts: 2.75 us -> none  [the longest x1 1.47 us: on_device(): targets[:, None]]
where the time goes in v2:
time: 207 us
  Pallas kernels  206 us (100%)
    pallas_call x1, Pallas kernels, core_call(): pl.pallas_call(functools.partial(core_kernel, ndp, nv), out_shape=(jax.Sh...  187 us
    pallas_call x1, Pallas kernels, head_grad_call(): pl.pallas_call(grad_kernel, grid=(wide // 256,), out_shape=jax.ShapeDtype...  11.4 us
    pallas_call x1, Pallas kernels, embed_grad_call(): pl.pallas_call(functools.partial(embed_kernel, vdev), grid=(wide // 256,)...  7.18 us

profile of v2, /device:TPU:7, one launch (start us, length us, event | category | flops | bytes accessed | tf_op | source)
XLA Modules:
  0.0 207.2 jit_solution(2904361452496627122)
XLA Ops:
  0.6 187.2 %core.1 = (bf16[4,256,1280]{2,1,0:T(8,128)(2,1)}, bf16[4,64,1280]{2,1,0:T(8,128)(2,1)}, bf16[4,256,2432]{2,1,0:T(8,128)(2,1)}, f32[4,64,128]{2,1,0:T(8,128)}, bf16[128,1280]{1,0:T(8,128)(2,1)}) custom-call(bf16[256,5120]{1,0:T(8,128)(2,1)} %hidden.1, bf16[256,5120]{1,0:T(8,128)(2,1)} %cot.1, bf16[1280,2432]{1,0:T(8,128)(2,1)} %head.1, s32[1,256]{1,0:T(1,128)} %bitcast.10, ...), custom_call_target="tpu_custom_call" | custom-call | tf_op jit(solution)/shard_map/core/pallas_call | solution.py:348
  187.8 11.4 %head_grad.1 = bf16[1280,2432]{1,0:T(8,128)(2,1)} custom-call(bf16[1024,1280]{1,0:T(8,128)(2,1)} %bitcast.7, bf16[1024,2432]{1,0:T(8,128)(2,1)} %bitcast.6), custom_call_target="tpu_custom_call" | custom-call | tf_op jit(solution)/shard_map/head_grad/pallas_call | solution.py:398
  199.3 0.0 copy-start
  199.3 7.2 %embed_grad.1 = bf16[1280,2432]{1,0:T(8,128)(2,1)} custom-call(bf16[256,1280]{1,0:T(8,128)(2,1)} %bitcast.8, f32[256,128]{1,0:T(8,128)} %bitcast.9), custom_call_target="tpu_custom_call" | custom-call | tf_op jit(solution)/shard_map/embed_grad/pallas_call | solution.py:423
  206.5 0.0 copy-done
  206.5 0.7 copy.9
Async XLA Ops:
  199.3 7.2 %copy-start = (bf16[128,1280]{1,0:T(8,128)(2,1)S(1)}, bf16[128,1280]{1,0:T(8,128)(2,1)}, u32[]{:S(2)}) copy-start(bf16[128,1280]{1,0:T(8,128)(2,1)} %get-tuple-element.18) | copy-start | bytes 983044
